TPU v7x, 128 devices: a whole 4x4x4 slice. The times are simulated.
128 devices in a mesh: fsdp: 32 (over x, z, core), tensor: 4 (over y).
Axes of the slice: x: 4, y: 4, z: 4, core: 2. Of those that a mesh axis runs over, the one named last changes fastest.
Arguments:
- tokens: bfloat16 [24576, 8192], P('fsdp'), may hold values from -6 to 6
- weight: bfloat16 [8192, 8192], P('fsdp', 'tensor'), may hold values from -0.0625 to 0.0625
- momentum: float32 [8192, 8192], P('fsdp', 'tensor'), may hold values from -700 to 700
- gradient: bfloat16 [8192, 8192], P('fsdp', 'tensor'), may hold values from -6 to 6
- probes: float32 [32, 8192], P(None, 'tensor'), may hold values from -6 to 6
Outputs:
- activations: float32 [24576, 8192], P('fsdp', 'tensor')
- momentum_out: float32 [8192, 8192], P('fsdp', 'tensor')
- krylov_scaled: float32 [96, 96], replicated
All inputs are finite; a program needn't handle non-finite values.
Results may differ from a plain program's by a relative error of at most 0.0029.
Values may be sent and summed in bfloat16 or wider, within the bound.
A program may use at most 192 MiB of HBM per device.

v0:
```python
import jax
import jax.numpy as jnp
from jax import lax
from jax.sharding import PartitionSpec as P

STEPS = 3
POWER = 32
highest = lax.Precision.HIGHEST
decay_factor = 0.9


def hdot(left, right):
    return jnp.dot(left, right, precision=highest, preferred_element_type=jnp.float32)


def orthonormal(block_mat, gram_mat):
    factor_low = jnp.linalg.cholesky(gram_mat)
    basis_next = jax.scipy.linalg.solve_triangular(factor_low, block_mat, lower=True)
    return (basis_next, factor_low)


def assemble(diag_blocks, low_factors):
    blk_width = diag_blocks[0].shape[0]
    total_size = len(diag_blocks) * blk_width
    krylov = jnp.zeros((total_size, total_size), jnp.float32)
    for position, diag_mat in enumerate(diag_blocks):
        first_at = position * blk_width
        krylov = krylov.at[first_at : first_at + blk_width, first_at : first_at + blk_width].set(
            diag_mat
        )
    for position, factor_low in enumerate(low_factors):
        first_at = position * blk_width
        second_at = first_at + blk_width
        krylov = krylov.at[second_at : second_at + blk_width, first_at:second_at].set(factor_low.T)
        krylov = krylov.at[first_at:second_at, second_at : second_at + blk_width].set(factor_low)
    return krylov


def top_value(krylov):

    def advance(position, vector):
        moved = hdot(krylov, vector)
        return moved / jnp.sqrt(jnp.sum(moved * moved))

    vector = lax.fori_loop(0, POWER, advance, jnp.ones((krylov.shape[0],), jnp.float32))
    return jnp.sum(vector * hdot(krylov, vector))


def local(tokens, weight, momentum, gradient, probes):
    moment = decay_factor * momentum + gradient.astype(jnp.float32)
    num_probes = probes.shape[0]

    def block_sum(values):
        return lax.psum(values, "tensor")

    basis_now, factor_first = orthonormal(probes, block_sum(hdot(probes, probes.T)))
    basis_prev = jnp.zeros_like(basis_now)
    low_prev = jnp.zeros((num_probes, num_probes), jnp.float32)
    diag_blocks = []
    low_factors = []
    for lanczos_step in range(STEPS):
        basis_full = basis_now
        reduced = lax.psum(hdot(basis_full, moment.T), "tensor")
        images = lax.psum(hdot(reduced, moment), "fsdp")
        diag_raw = block_sum(hdot(basis_now, images.T))
        diag_mat = 0.5 * (diag_raw + diag_raw.T)
        diag_blocks.append(diag_mat)
        if lanczos_step + 1 < STEPS:
            residue = images - hdot(diag_mat, basis_now) - hdot(low_prev.T, basis_prev)
            basis_next, factor_low = orthonormal(residue, block_sum(hdot(residue, residue.T)))
            low_factors.append(factor_low)
            basis_prev, low_prev, basis_now = (basis_now, factor_low, basis_next)
    krylov = assemble(diag_blocks, low_factors)
    top = top_value(krylov)
    new_weight = (weight.astype(jnp.float32) - moment / jnp.sqrt(top)).astype(jnp.bfloat16)
    summed = jnp.dot(
        tokens,
        lax.all_gather(new_weight, "fsdp", axis=0, tiled=True),
        preferred_element_type=jnp.float32,
    )
    return (summed, moment, krylov / top)


def solution(mesh):
    return jax.shard_map(
        local,
        mesh=mesh,
        in_specs=(
            P("fsdp", None),
            P("fsdp", "tensor"),
            P("fsdp", "tensor"),
            P("fsdp", "tensor"),
            P(None, "tensor"),
        ),
        out_specs=(P("fsdp", "tensor"), P("fsdp", "tensor"), P()),
        check_vma=False,
    )
```

profile of v0, /device:TPU:1, one launch (start us, length us, event | category | flops | bytes accessed | tf_op | source)
XLA Modules:
  0.0 754.3 jit_solution(2024428877943884364)
XLA Ops:
  8.5 14.2 %psum.84 = f32[32,32]{0,1:T(8,128)S(1)} all-reduce(f32[32,32]{0,1:T(8,128)S(1)} %fusion.24), channel_id=1, replica_groups=mesh['fsdp'=32,'tensor'=4] {'tensor'}, use_global_device_ids=true, to_apply=%region_0.0 | all-reduce | flops 1024 | bytes 8192 | tf_op jit(solution)/shard_map/psum | solution.py:54
  22.8 2.9 cholesky.59
  27.0 2.4 custom-call.8
  29.9 2.3 convert_add_fusion
  32.3 1.9 fusion.25
  34.2 11.1 %psum.85 = f32[32,256]{1,0:T(8,128)S(1)} all-reduce(f32[32,256]{1,0:T(8,128)S(1)} %fusion.25), channel_id=1, replica_groups=mesh['fsdp'=32,'tensor'=4] {'tensor'}, use_global_device_ids=true, to_apply=%region_3.0 | all-reduce | flops 8192 | bytes 65536 | tf_op jit(solution)/shard_map/psum | solution.py:63
  45.3 2.0 fusion.26
  47.4 109.7 %all-reduce.5.cloned.1.call-done = f32[32,2048]{1,0:T(8,128)} async-done(((f32[32,2048]{1,0:T(8,128)}), f32[32,2048]{1,0:T(8,128)}) %all-reduce.5.cloned.1.call-update) | async-done | bytes 262160 | tf_op jit(solution)/shard_map/psum | solution.py:64
  158.4 13.1 %psum.87 = f32[32,32]{0,1:T(8,128)S(1)} all-reduce(f32[32,32]{0,1:T(8,128)S(1)} %fusion.27), channel_id=1, replica_groups=mesh['fsdp'=32,'tensor'=4] {'tensor'}, use_global_device_ids=true, to_apply=%region_5.0 | all-reduce | flops 1024 | bytes 8192 | tf_op jit(solution)/shard_map/psum | solution.py:54
  173.6 11.1 %psum.88 = f32[32,32]{0,1:T(8,128)S(1)} all-reduce(f32[32,32]{0,1:T(8,128)S(1)} %fusion.28), channel_id=1, replica_groups=mesh['fsdp'=32,'tensor'=4] {'tensor'}, use_global_device_ids=true, to_apply=%region_6.0 | all-reduce | flops 1024 | bytes 8192 | tf_op jit(solution)/shard_map/psum | solution.py:54
  184.7 2.9 cholesky.70
  188.9 2.4 custom-call.9
  191.8 1.9 fusion.29
  193.8 11.3 %psum.89 = f32[32,256]{1,0:T(8,128)S(1)} all-reduce(f32[32,256]{1,0:T(8,128)S(1)} %fusion.29), channel_id=1, replica_groups=mesh['fsdp'=32,'tensor'=4] {'tensor'}, use_global_device_ids=true, to_apply=%region_7.0 | all-reduce | flops 8192 | bytes 65536 | tf_op jit(solution)/shard_map/psum | solution.py:63
  205.1 2.0 fusion.30
  207.2 110.4 %all-reduce.7.cloned.1.call-done = f32[32,2048]{1,0:T(8,128)} async-done(((f32[32,2048]{1,0:T(8,128)}), f32[32,2048]{1,0:T(8,128)}) %all-reduce.7.cloned.1.call-update) | async-done | bytes 262160 | tf_op jit(solution)/shard_map/psum | solution.py:64
  318.9 13.1 %psum.91 = f32[32,32]{0,1:T(8,128)S(1)} all-reduce(f32[32,32]{0,1:T(8,128)S(1)} %fusion.31), channel_id=1, replica_groups=mesh['fsdp'=32,'tensor'=4] {'tensor'}, use_global_device_ids=true, to_apply=%region_9.0 | all-reduce | flops 1024 | bytes 8192 | tf_op jit(solution)/shard_map/psum | solution.py:54
  334.2 11.2 %psum.92 = f32[32,32]{0,1:T(8,128)S(1)} all-reduce(f32[32,32]{0,1:T(8,128)S(1)} %fusion.32), channel_id=1, replica_groups=mesh['fsdp'=32,'tensor'=4] {'tensor'}, use_global_device_ids=true, to_apply=%region_10.0 | all-reduce | flops 1024 | bytes 8192 | tf_op jit(solution)/shard_map/psum | solution.py:54
  345.5 2.9 cholesky.81
  349.7 2.4 custom-call.10
  352.6 1.9 fusion.33
  354.5 11.1 %psum.93 = f32[32,256]{1,0:T(8,128)S(1)} all-reduce(f32[32,256]{1,0:T(8,128)S(1)} %fusion.33), channel_id=1, replica_groups=mesh['fsdp'=32,'tensor'=4] {'tensor'}, use_global_device_ids=true, to_apply=%region_11.0 | all-reduce | flops 8192 | bytes 65536 | tf_op jit(solution)/shard_map/psum | solution.py:63
  365.7 2.0 fusion.34
  370.1 108.0 %all-reduce.9.cloned.1.call-done = f32[32,2048]{1,0:T(8,128)} async-done(((f32[32,2048]{1,0:T(8,128)}), f32[32,2048]{1,0:T(8,128)}) %all-reduce.9.cloned.1.call-update) | async-done | bytes 262160 | tf_op jit(solution)/shard_map/psum | solution.py:64
  479.5 13.1 %psum.95 = f32[32,32]{0,1:T(8,128)S(1)} all-reduce(f32[32,32]{0,1:T(8,128)S(1)} %fusion.35), channel_id=1, replica_groups=mesh['fsdp'=32,'tensor'=4] {'tensor'}, use_global_device_ids=true, to_apply=%region_13.0 | all-reduce | flops 1024 | bytes 8192 | tf_op jit(solution)/shard_map/psum | solution.py:54
  494.2 1.9 dynamic-slice_select_fusion
  496.1 2.1 scatter.30
  500.0 87.1 %while.18 = (s32[]{:T(128)}, f32[96]{0:T(128)}, f32[96,96]{1,0:T(8,128)S(1)}, s32[]{:T(128)}, s32[]{:T(128)}) while((s32[]{:T(128)}, f32[96]{0:T(128)}, f32[96,96]{1,0:T(8,128)S(1)}, s32[]{:T(128)}, s32[]{:T(128)}) %tuple.63), condition=%wide.region_17.0_spmd.clone, body=%wide.region_15.19_spmd.clone.sunk | while | flops 110978 | bytes 38487 | solution.py:45
  502.1 1.5 multiply_reduce_fusion.2
  504.8 1.5 multiply_reduce_fusion.2
  507.5 1.5 multiply_reduce_fusion.2
  510.3 1.5 multiply_reduce_fusion.2
  513.0 1.5 multiply_reduce_fusion.2
  515.8 1.5 multiply_reduce_fusion.2
  518.5 1.5 multiply_reduce_fusion.2
  521.2 1.5 multiply_reduce_fusion.2
  524.0 1.5 multiply_reduce_fusion.2
  526.7 1.5 multiply_reduce_fusion.2
  529.5 1.5 multiply_reduce_fusion.2
  532.2 1.5 multiply_reduce_fusion.2
  535.0 1.5 multiply_reduce_fusion.2
  537.7 1.5 multiply_reduce_fusion.2
  540.4 1.5 multiply_reduce_fusion.2
  543.2 1.5 multiply_reduce_fusion.2
  545.9 1.5 multiply_reduce_fusion.2
  548.7 1.5 multiply_reduce_fusion.2
  551.4 1.5 multiply_reduce_fusion.2
  554.1 1.5 multiply_reduce_fusion.2
  556.9 1.5 multiply_reduce_fusion.2
  559.6 1.5 multiply_reduce_fusion.2
  562.4 1.5 multiply_reduce_fusion.2
  565.1 1.5 multiply_reduce_fusion.2
  567.8 1.5 multiply_reduce_fusion.2
  570.6 1.5 multiply_reduce_fusion.2
  573.3 1.5 multiply_reduce_fusion.2
  576.1 1.5 multiply_reduce_fusion.2
  578.8 1.5 multiply_reduce_fusion.2
  581.6 1.5 multiply_reduce_fusion.2
  584.3 1.5 multiply_reduce_fusion.2
  587.0 1.6 fusion.5
  590.7 1.3 broadcast_divide_fusion.1
  592.0 114.0 %all-gather.2.cloned.1.call-done = bf16[8192,2048]{1,0:T(8,128)(2,1)} async-done(((bf16[256,2048]{1,0:T(8,128)(2,1)}), bf16[8192,2048]{1,0:T(8,128)(2,1)}) %all-gather.2.cloned.1.call-update) | async-done | bytes 33554448 | tf_op jit(solution)/shard_map/all_gather | solution.py:78
  705.9 35.2 %convolution_bitcast_fusion.1 = f32[768,2048]{0,1:T(8,128)} fusion(bf16[8192,2048]{1,0:T(8,128)(2,1)} %all-gather.2.cloned.1.call-done, bf16[768,8192]{1,0:T(8,128)(2,1)} %param.24), kind=kOutput, calls=%fused_computation.7 | convolution fusion | flops 25769803776 | bytes 52428800 | tf_op jit(solution)/shard_map/dot_general | solution.py:76
  741.1 6.6 copy.22
  (96 shorter events, 41.3 us)
Async XLA Ops:
  7.2 1.0 copy-start
  7.2 149.9 %all-reduce.5.cloned.1.call-start = ((), (), s32[]{:S(2)}) async-start(), calls=%async_computation | async-start | bytes 524288 | tf_op jit(solution)/shard_map/psum | solution.py:64
  32.2 557.1 %copy-start.2 = (f32[256,2048]{1,0:T(8,128)}, f32[256,2048]{1,0:T(8,128)S(1)}, u32[]{:S(2)}) copy-start(f32[256,2048]{1,0:T(8,128)S(1)} %convert_add_fusion) | copy-start | bytes 6291460
  47.3 270.2 %all-reduce.7.cloned.1.call-start = ((), (), s32[]{:S(2)}) async-start(), calls=%async_computation.1 | async-start | bytes 524288 | tf_op jit(solution)/shard_map/psum | solution.py:64
  207.1 271.1 %all-reduce.9.cloned.1.call-start = ((), (), s32[]{:S(2)}) async-start(), calls=%async_computation.2 | async-start | bytes 524288 | tf_op jit(solution)/shard_map/psum | solution.py:64
  365.7 223.7 %copy-start.3 = (bf16[256,2048]{1,0:T(8,128)(2,1)S(1)}, bf16[256,2048]{1,0:T(8,128)(2,1)}, u32[]{:S(2)}) copy-start(bf16[256,2048]{1,0:T(8,128)(2,1)} %param.25) | copy-start | bytes 3145732
  367.7 338.2 %all-gather.2.cloned.1.call-start = ((), (), s32[]{:S(2)}) async-start(), calls=%async_computation.3 | async-start | bytes 34603008 | tf_op jit(solution)/shard_map/all_gather | solution.py:78
  741.1 6.6 copy-start.1
Sparse Core Ops, SparseCore 0:
  47.5 109.6 all-reduce.4
  207.2 110.2 all-reduce.6
  367.8 110.2 all-reduce.8
  590.8 115.0 all-gather.1
where the time goes:
time: 755 us; the launch traced here: 754 us
  waiting for transfers between devices  442 us (59%)
  blocking collectives  109 us (14%)
  matrix products  104 us (14%)
  other arithmetic  46.2 us (6%)
  loops' own time  22.2 us (3%)
  local copies, waits for them, and re-layouts  14.9 us (2%)
  between operations  14.8 us (2%)
    psum x3, waiting for transfers between devices, local(): images = lax.psum(hdot(reduced, moment), 'fsdp')  328 us
    all_gather x1, waiting for transfers between devices, local(): lax.all_gather(new_weight, 'fsdp', axis=0, tiled=True)  114 us
    psum x6, blocking collectives, block_sum(): return lax.psum(values, 'tensor')  75.9 us
    dot_general x49, matrix products, hdot(): jnp.dot(left, right, precision=highest, preferred_element_type=jnp.float32)  67.9 us
    dot_general x1, matrix products, local(): jnp.dot(tokens, lax.all_gather(new_weight, 'fsdp', axis=0, tiled=True), p...  35.2 us
    psum x3, blocking collectives, local(): reduced = lax.psum(hdot(basis_full, moment.T), 'tensor')  33.5 us
    another operation x1, loops' own time, top_value(): lax.fori_loop(0, POWER, advance, jnp.ones((krylov.shape[0],), jnp.float32))  22.2 us
    div x32, other arithmetic, advance(): return moved / jnp.sqrt(jnp.sum(moved * moved))  18.6 us
  transfers between devices with their start and end apart: 4, of which 4 were waited for; matrix products, arithmetic and copies ran while one was open for 0% of the time, Pallas kernels for 0%

commit v1 on v0

--- a/solution.py
+++ b/solution.py
@@ -7,6 +7,11 @@
 POWER = 32
 highest = lax.Precision.HIGHEST
 decay_factor = 0.9
+
+
+def all_by_exchange(array, name, d):
+    outgoing = jnp.stack([array] * lax.axis_size(name))
+    return jnp.concatenate(lax.all_to_all(outgoing, name, 0, 0), axis=d)
 
 
 def hdot(left, right):
@@ -74,9 +79,7 @@
     top = top_value(krylov)
     new_weight = (weight.astype(jnp.float32) - moment / jnp.sqrt(top)).astype(jnp.bfloat16)
     summed = jnp.dot(
-        tokens,
-        lax.all_gather(new_weight, "fsdp", axis=0, tiled=True),
-        preferred_element_type=jnp.float32,
+        tokens, all_by_exchange(new_weight, "fsdp", 0), preferred_element_type=jnp.float32
     )
     return (summed, moment, krylov / top)
 

time: 755 us -> 1210 us (1.60)
  the two profiles are of different devices: /device:TPU:1 before, /device:TPU:36 now
where the time goes in v1:
time: 1210 us
  waiting for transfers between devices  845 us (70%)
  blocking collectives  142 us (12%)
  matrix products  104 us (9%)
  other arithmetic  45.2 us (4%)
  local copies, waits for them, and re-layouts  25.9 us (2%)
  loops' own time  22.2 us (2%)
  between operations  14.8 us (1%)
    all_to_all x1, waiting for transfers between devices, all_by_exchange(): return jnp.concatenate(lax.all_to_all(outgoing, name, 0, 0), axis=d)  548 us
    psum x3, waiting for transfers between devices, local(): images = lax.psum(hdot(reduced, moment), 'fsdp')  297 us
    psum x6, blocking collectives, block_sum(): return lax.psum(values, 'tensor')  96.5 us
    dot_general x49, matrix products, hdot(): jnp.dot(left, right, precision=highest, preferred_element_type=jnp.float32)  67.8 us
    psum x3, blocking collectives, local(): reduced = lax.psum(hdot(basis_full, moment.T), 'tensor')  45.5 us
    dot_general x1, matrix products, local(): jnp.dot(tokens, all_by_exchange(new_weight, 'fsdp', 0), preferred_element...  35.2 us
  transfers between devices with their start and end apart: 4, of which 4 were waited for; matrix products, arithmetic and copies ran while one was open for 0% of the time, Pallas kernels for 0%

profile of v1, /device:TPU:36, one launch (start us, length us, event | category | flops | bytes accessed | tf_op | source)
XLA Modules:
  0.0 1206.2 jit_solution(8497625098727673682)
XLA Ops:
  8.5 17.2 %psum.84 = f32[32,32]{0,1:T(8,128)S(1)} all-reduce(f32[32,32]{0,1:T(8,128)S(1)} %fusion.24), channel_id=1, replica_groups=mesh['fsdp'=32,'tensor'=4] {'tensor'}, use_global_device_ids=true, to_apply=%region_0.0 | all-reduce | flops 1024 | bytes 8192 | tf_op jit(solution)/shard_map/psum | solution.py:59
  25.7 2.9 cholesky.59
  30.0 2.4 custom-call.8
  32.9 2.3 convert_add_fusion
  35.2 1.9 fusion.25
  37.1 14.4 %psum.85 = f32[32,256]{1,0:T(8,128)S(1)} all-reduce(f32[32,256]{1,0:T(8,128)S(1)} %fusion.25), channel_id=1, replica_groups=mesh['fsdp'=32,'tensor'=4] {'tensor'}, use_global_device_ids=true, to_apply=%region_3.0 | all-reduce | flops 8192 | bytes 65536 | tf_op jit(solution)/shard_map/psum | solution.py:68
  51.6 2.0 fusion.26
  53.6 101.1 %all-reduce.5.cloned.1.call-done = f32[32,2048]{1,0:T(8,128)} async-done(((f32[32,2048]{1,0:T(8,128)}), f32[32,2048]{1,0:T(8,128)}) %all-reduce.5.cloned.1.call-update) | async-done | bytes 262160 | tf_op jit(solution)/shard_map/psum | solution.py:69
  156.0 16.9 %psum.87 = f32[32,32]{0,1:T(8,128)S(1)} all-reduce(f32[32,32]{0,1:T(8,128)S(1)} %fusion.27), channel_id=1, replica_groups=mesh['fsdp'=32,'tensor'=4] {'tensor'}, use_global_device_ids=true, to_apply=%region_5.0 | all-reduce | flops 1024 | bytes 8192 | tf_op jit(solution)/shard_map/psum | solution.py:59
  174.9 14.3 %psum.88 = f32[32,32]{0,1:T(8,128)S(1)} all-reduce(f32[32,32]{0,1:T(8,128)S(1)} %fusion.28), channel_id=1, replica_groups=mesh['fsdp'=32,'tensor'=4] {'tensor'}, use_global_device_ids=true, to_apply=%region_6.0 | all-reduce | flops 1024 | bytes 8192 | tf_op jit(solution)/shard_map/psum | solution.py:59
  189.2 2.9 cholesky.70
  193.5 2.4 custom-call.9
  196.4 1.9 fusion.29
  198.3 15.6 %psum.89 = f32[32,256]{1,0:T(8,128)S(1)} all-reduce(f32[32,256]{1,0:T(8,128)S(1)} %fusion.29), channel_id=1, replica_groups=mesh['fsdp'=32,'tensor'=4] {'tensor'}, use_global_device_ids=true, to_apply=%region_7.0 | all-reduce | flops 8192 | bytes 65536 | tf_op jit(solution)/shard_map/psum | solution.py:68
  213.9 2.0 fusion.30
  216.0 99.1 %all-reduce.7.cloned.1.call-done = f32[32,2048]{1,0:T(8,128)} async-done(((f32[32,2048]{1,0:T(8,128)}), f32[32,2048]{1,0:T(8,128)}) %all-reduce.7.cloned.1.call-update) | async-done | bytes 262160 | tf_op jit(solution)/shard_map/psum | solution.py:69
  316.4 16.9 %psum.91 = f32[32,32]{0,1:T(8,128)S(1)} all-reduce(f32[32,32]{0,1:T(8,128)S(1)} %fusion.31), channel_id=1, replica_groups=mesh['fsdp'=32,'tensor'=4] {'tensor'}, use_global_device_ids=true, to_apply=%region_9.0 | all-reduce | flops 1024 | bytes 8192 | tf_op jit(solution)/shard_map/psum | solution.py:59
  335.5 14.5 %psum.92 = f32[32,32]{0,1:T(8,128)S(1)} all-reduce(f32[32,32]{0,1:T(8,128)S(1)} %fusion.32), channel_id=1, replica_groups=mesh['fsdp'=32,'tensor'=4] {'tensor'}, use_global_device_ids=true, to_apply=%region_10.0 | all-reduce | flops 1024 | bytes 8192 | tf_op jit(solution)/shard_map/psum | solution.py:59
  350.0 2.9 cholesky.81
  354.3 2.4 custom-call.10
  357.2 1.9 fusion.33
  359.1 15.4 %psum.93 = f32[32,256]{1,0:T(8,128)S(1)} all-reduce(f32[32,256]{1,0:T(8,128)S(1)} %fusion.33), channel_id=1, replica_groups=mesh['fsdp'=32,'tensor'=4] {'tensor'}, use_global_device_ids=true, to_apply=%region_11.0 | all-reduce | flops 8192 | bytes 65536 | tf_op jit(solution)/shard_map/psum | solution.py:68
  374.5 2.0 fusion.34
  378.9 96.8 %all-reduce.9.cloned.1.call-done = f32[32,2048]{1,0:T(8,128)} async-done(((f32[32,2048]{1,0:T(8,128)}), f32[32,2048]{1,0:T(8,128)}) %all-reduce.9.cloned.1.call-update) | async-done | bytes 262160 | tf_op jit(solution)/shard_map/psum | solution.py:69
  477.1 16.9 %psum.95 = f32[32,32]{0,1:T(8,128)S(1)} all-reduce(f32[32,32]{0,1:T(8,128)S(1)} %fusion.35), channel_id=1, replica_groups=mesh['fsdp'=32,'tensor'=4] {'tensor'}, use_global_device_ids=true, to_apply=%region_13.0 | all-reduce | flops 1024 | bytes 8192 | tf_op jit(solution)/shard_map/psum | solution.py:59
  495.5 1.9 dynamic-slice_select_fusion
  497.4 2.1 scatter.30
  501.3 87.1 %while.18 = (s32[]{:T(128)}, f32[96]{0:T(128)}, f32[96,96]{1,0:T(8,128)S(1)}, s32[]{:T(128)}, s32[]{:T(128)}) while((s32[]{:T(128)}, f32[96]{0:T(128)}, f32[96,96]{1,0:T(8,128)S(1)}, s32[]{:T(128)}, s32[]{:T(128)}) %tuple.63), condition=%wide.region_17.0_spmd.clone, body=%wide.region_15.19_spmd.clone.sunk | while | flops 110978 | bytes 38487 | solution.py:50
  503.4 1.5 multiply_reduce_fusion.2
  506.1 1.5 multiply_reduce_fusion.2
  508.9 1.5 multiply_reduce_fusion.2
  511.6 1.5 multiply_reduce_fusion.2
  514.4 1.5 multiply_reduce_fusion.2
  517.1 1.5 multiply_reduce_fusion.2
  519.8 1.5 multiply_reduce_fusion.2
  522.6 1.5 multiply_reduce_fusion.2
  525.3 1.5 multiply_reduce_fusion.2
  528.1 1.5 multiply_reduce_fusion.2
  530.8 1.5 multiply_reduce_fusion.2
  533.5 1.5 multiply_reduce_fusion.2
  536.3 1.5 multiply_reduce_fusion.2
  539.0 1.5 multiply_reduce_fusion.2
  541.8 1.5 multiply_reduce_fusion.2
  544.5 1.5 multiply_reduce_fusion.2
  547.2 1.5 multiply_reduce_fusion.2
  550.0 1.5 multiply_reduce_fusion.2
  552.7 1.5 multiply_reduce_fusion.2
  555.5 1.5 multiply_reduce_fusion.2
  558.2 1.5 multiply_reduce_fusion.2
  561.0 1.5 multiply_reduce_fusion.2
  563.7 1.5 multiply_reduce_fusion.2
  566.4 1.5 multiply_reduce_fusion.2
  569.2 1.5 multiply_reduce_fusion.2
  571.9 1.5 multiply_reduce_fusion.2
  574.7 1.5 multiply_reduce_fusion.2
  577.4 1.5 multiply_reduce_fusion.2
  580.1 1.5 multiply_reduce_fusion.2
  582.9 1.5 multiply_reduce_fusion.2
  588.4 1.5 fusion.5
  590.9 11.0 stack.2
  602.0 7.0 all-to-all-start
  610.2 547.7 %all-to-all-done = bf16[32,256,2048]{2,1,0:T(8,128)(2,1)} async-done(((bf16[32,256,2048]{2,1,0:T(8,128)(2,1)}), bf16[32,256,2048]{2,1,0:T(8,128)(2,1)}, u32[]{:S(2)}, u32[]{:S(2)}) %all-to-all-start) | async-done | bytes 33554464 | tf_op jit(solution)/shard_map/all_to_all | solution.py:14
  1157.9 35.2 %convolution_bitcast_fusion.1 = f32[768,2048]{0,1:T(8,128)} fusion(bf16[8192,2048]{1,0:T(8,128)(2,1)} %bitcast.18, bf16[768,8192]{1,0:T(8,128)(2,1)} %param.24), kind=kOutput, calls=%fused_computation.7 | convolution fusion | flops 25769803776 | bytes 52428800 | tf_op jit(solution)/shard_map/dot_general | solution.py:81
  1193.1 6.6 copy.22
  (96 shorter events, 43.0 us)
Async XLA Ops:
  7.2 1.0 copy-start
  7.2 147.5 %all-reduce.5.cloned.1.call-start = ((), (), s32[]{:S(2)}) async-start(), calls=%async_computation.1 | async-start | bytes 524288 | tf_op jit(solution)/shard_map/psum | solution.py:69
  35.2 555.4 %copy-start.2 = (f32[256,2048]{1,0:T(8,128)}, f32[256,2048]{1,0:T(8,128)S(1)}, u32[]{:S(2)}) copy-start(f32[256,2048]{1,0:T(8,128)S(1)} %convert_add_fusion) | copy-start | bytes 6291460
  53.6 261.5 %all-reduce.7.cloned.1.call-start = ((), (), s32[]{:S(2)}) async-start(), calls=%async_computation.2 | async-start | bytes 524288 | tf_op jit(solution)/shard_map/psum | solution.py:69
  216.0 259.8 %all-reduce.9.cloned.1.call-start = ((), (), s32[]{:S(2)}) async-start(), calls=%async_computation.3 | async-start | bytes 524288 | tf_op jit(solution)/shard_map/psum | solution.py:69
  374.5 216.1 %copy-start.3 = (bf16[256,2048]{1,0:T(8,128)(2,1)S(1)}, bf16[256,2048]{1,0:T(8,128)(2,1)}, u32[]{:S(2)}) copy-start(bf16[256,2048]{1,0:T(8,128)(2,1)} %param.25) | copy-start | bytes 3145732
  602.0 555.9 %all-to-all-start = ((bf16[32,256,2048]{2,1,0:T(8,128)(2,1)}), bf16[32,256,2048]{2,1,0:T(8,128)(2,1)}, u32[]{:S(2)}, u32[]{:S(2)}) async-start(bf16[32,256,2048]{2,1,0:T(8,128)(2,1)} %stack.2), calls=%async_computation | async-start | bytes 67108864 | tf_op jit(solution)/shard_map/all_to_all | solution.py:14
  1193.1 6.6 copy-start.1
Sparse Core Ops, SparseCore 0:
  53.7 100.9 all-reduce.4
  216.1 98.9 all-reduce.6
  376.7 99.0 all-reduce.8
